TPU v7x, 256 devices: a whole 4x4x8 slice. The times are simulated.
256 devices in a mesh: row: 8 (over z), col: 16 (over y, x), pan: 2 (over core).
Axes of the slice: x: 4, y: 4, z: 8, core: 2. Of those that a mesh axis runs over, the one named last changes fastest.
Arguments:
- plan_values: bfloat16 [8192, 128, 256], P('row', 'col', 'pan'), may hold values from 0.099609375 to 1
- plan_blocks: int32 [8, 128], P('row', 'col'), may hold values from 0 to 127, as said below
- first_values: bfloat16 [32, 3, 256, 256], P('row'), may hold values from -0.21875 to 0.21875
- first_blocks: int32 [32, 3], P('row'), may hold values from 0 to 3, as said below
- second_values: bfloat16 [128, 6, 256, 256], P('col', None, None, 'pan'), may hold values from -0.15625 to 0.15625
- second_blocks: int32 [128, 6], P('col'), may hold values from 0 to 7, as said below
- weight_first: float32 [8192], P('row'), may hold values from 0.5 to 2
- weight_second: float32 [128, 256], P('col', 'pan'), may hold values from 0.5 to 2
- offset_first: float32 [8192], P('row'), may hold values from -3 to 3
- offset_second: float32 [128, 256], P('col', 'pan'), may hold values from -3 to 3
Outputs:
- new_plan: bfloat16 [8192, 128, 256], P('row', 'col', 'pan')
- scale_first: float32 [8192], P('row')
- scale_second: float32 [128, 256], P('col', 'pan')
Inputs may be any that keep to these rules, and one draw needn't show every extreme that they name: `plan_blocks`: each entry is a slice-B block number; its column panel is the entry // 8. Within the 8 slots of one index of col (aligned groups of the second dimension) no column panel is named more than 2 times, and in every row panel one column panel is named exactly 2 times by every such group. `first_blocks`: block numbers within the row panel of the slice-A block; the 3 entries of a row are distinct. `second_blocks`: block numbers within the column panel of the slice-B block; the 6 entries of a row are distinct.
All inputs are finite; a program needn't handle non-finite values.
Results may differ from a plain program's by a relative error of at most 0.0087.
Values may be sent and summed in bfloat16 or wider, within the bound.
No kernel may reach another device: no remote copies, remote signals or barrier semaphores. Data moves between devices by JAX's collectives and lax.ppermute only.
A program may use at most 128 MiB of HBM per device.

v0:
```python
import jax
import jax.numpy as jnp
from jax import lax
from jax.sharding import PartitionSpec as P

CAP = 2


def first_product(plan_values, first_values, first_blocks):
    tile_count = first_blocks.shape[0]
    block_size = first_values.shape[2]
    slot_count = plan_values.shape[1]
    half_width = plan_values.shape[2]
    row_tiles = plan_values.reshape(tile_count, block_size, slot_count * half_width)
    running = jnp.zeros(row_tiles.shape, jnp.float32)
    for neighbor in range(first_blocks.shape[1]):
        picked = jnp.take(row_tiles, first_blocks[:, neighbor], axis=0)
        running = running + jnp.einsum(
            "iab,ibn->ian", first_values[:, neighbor], picked, preferred_element_type=jnp.float32
        )
    return running.astype(jnp.bfloat16).reshape(tile_count * block_size, slot_count, half_width)


def dispatch(chooser, within_panel, product):
    outgoing = jnp.einsum(
        "dcs,rsh->dcrh", chooser.astype(jnp.bfloat16), product, preferred_element_type=jnp.float32
    ).astype(jnp.bfloat16)
    labels = jnp.sum(chooser.astype(jnp.int32) * (within_panel + 1)[None, None, :], axis=2) - 1
    return (outgoing, labels)


def second_product(dense_plan, second_values, second_blocks):
    blocks_here = second_blocks.shape[0]
    columns = jnp.arange(blocks_here)
    placer = (second_blocks[:, :, None] == columns[None, None, :]).astype(jnp.bfloat16)
    panel_matrix = jnp.einsum(
        "kqbh,kql->kblh", second_values, placer, preferred_element_type=jnp.float32
    ).astype(jnp.bfloat16)
    return jnp.einsum("rkb,kblh->rlh", dense_plan, panel_matrix, preferred_element_type=jnp.float32)


def local(
    plan_values,
    plan_blocks,
    first_values,
    first_blocks,
    second_values,
    second_blocks,
    weight_first,
    weight_second,
    offset_first,
    offset_second,
):
    col_count = lax.axis_size("col")
    blocks_here = second_blocks.shape[0]
    slot_count = plan_values.shape[1]
    block_size = first_values.shape[2]
    panel_rows = plan_values.shape[0]
    plan_width = float(slot_count * col_count * block_size)
    named_blocks = plan_blocks[0]
    target_panel = named_blocks // blocks_here
    within_panel = named_blocks % blocks_here
    same_panel = target_panel[:, None] == target_panel[None, :]
    earlier = jnp.arange(slot_count)[:, None] > jnp.arange(slot_count)[None, :]
    position = jnp.sum((same_panel & earlier).astype(jnp.int32), axis=1)
    chooser = (target_panel[None, None, :] == jnp.arange(col_count)[:, None, None]) & (
        position[None, None, :] == jnp.arange(CAP)[None, :, None]
    )
    product = first_product(plan_values, first_values, first_blocks)
    outgoing, labels = dispatch(chooser, within_panel, product)
    incoming, arrival_ids = (
        lax.all_to_all(outgoing, "col", split_axis=0, concat_axis=0, tiled=True),
        lax.all_to_all(labels, "col", split_axis=0, concat_axis=0, tiled=True),
    )
    item_rows = incoming.shape[2]
    arrivals = incoming.reshape(col_count * CAP, item_rows, incoming.shape[3])
    matcher = (arrival_ids.reshape(-1)[:, None] == jnp.arange(blocks_here)[None, :]).astype(
        jnp.bfloat16
    )
    dense_plan = jnp.einsum(
        "ik,irh->rkh", matcher, arrivals, preferred_element_type=jnp.float32
    ).astype(jnp.bfloat16)
    present = jnp.minimum(jnp.sum(matcher.astype(jnp.float32), axis=0), 1.0)
    gathered = lax.all_gather(dense_plan, "pan", axis=2, tiled=True)
    crossed = second_product(gathered, second_values, second_blocks)
    kernel_values = present[None, :, None] * jnp.exp(
        crossed - offset_first[:, None, None] - offset_second[None]
    )
    row_totals = lax.psum(jnp.sum(kernel_values, axis=(1, 2)), ("col", "pan"))
    scale_first = weight_first * plan_width / row_totals
    weighted = kernel_values * scale_first[:, None, None]
    colsum, counts = lax.psum((jnp.sum(weighted, axis=0), present * float(panel_rows)), "row")
    scale_second = weight_second * counts[:, None] / jnp.where(counts[:, None] > 0, colsum, 1.0)
    new_values = (weighted * scale_second[None]).astype(jnp.bfloat16)
    returned = jnp.einsum(
        "ik,rkh->irh", matcher, new_values, preferred_element_type=jnp.float32
    ).astype(jnp.bfloat16)
    returned = returned.reshape(col_count, CAP, item_rows, returned.shape[2])
    homeward = lax.all_to_all(returned, "col", split_axis=0, concat_axis=0, tiled=True)
    new_plan = jnp.einsum(
        "dcs,dcrh->rsh", chooser.astype(jnp.bfloat16), homeward, preferred_element_type=jnp.float32
    ).astype(jnp.bfloat16)
    return (new_plan, scale_first, scale_second)


def solution(mesh):
    return jax.shard_map(
        local,
        mesh=mesh,
        in_specs=(
            P("row", "col", "pan"),
            P("row", "col"),
            P("row", None, None, None),
            P("row", None),
            P("col", None, None, "pan"),
            P("col", None),
            P("row"),
            P("col", "pan"),
            P("row"),
            P("col", "pan"),
        ),
        out_specs=(P("row", "col", "pan"), P("row"), P("col", "pan")),
        check_vma=False,
    )
```

profile of v0, /device:TPU:2, one launch (start us, length us, event | category | flops | bytes accessed | tf_op | source)
XLA Modules:
  0.0 442.7 jit_solution(4532502949180978923)
XLA Ops:
  7.2 0.0 copy-start
  7.2 0.8 fusion.59
  8.0 0.8 fusion.60
  8.8 0.1 iota_compare_fusion.3
  8.9 0.2 convert_reduce_fusion.1
  9.1 0.1 fusion.47
  9.2 0.7 copy.46
  9.8 7.5 %all-to-all-start = ((s32[16,1,2]{2,1,0:T(1,128)}), s32[16,1,2]{2,1,0:T(1,128)S(1)}, u32[]{:S(2)}, u32[]{:S(2)}) async-start(s32[16,1,2]{2,1,0:T(1,128)} %copy.46), calls=%async_computation | async-start | bytes 16384 | tf_op jit(solution)/shard_map/all_to_all | solution.py:73
  17.3 1.0 slice_reduce_fusion.1
  18.4 4.2 reshape.172
  22.6 3.6 gather_fusion.1
  26.1 3.6 gather_fusion.2
  29.7 3.6 gather_fusion
  33.3 2.8 fusion.20
  36.2 1.0 fusion.22
  37.3 0.5 copy-done.2
  37.8 2.7 fusion.29
  40.5 4.0 copy.53
  44.5 2.2 copy.72
  46.7 5.1 %convolution_convert_fusion.1 = bf16[16,2,1024,128]{3,0,2,1:T(8,128)(2,1)} fusion(bf16[1024,8,128,1]{2,1,0,3:T(8,128)(2,1)S(1)} %bitcast.93, pred[2,8]{1,0:T(4,128)(4,1)S(1)} %iota_compare_fusion.4, pred[16,8]{0,1:T(8,128)(4,1)S(1)} %iota_compare_fusion.3), kind=kOutput, calls=%fused_computation.8 | convolution fusion | flops 71303424 | bytes 10485904 | tf_op jit(solution)/shard_map/dcs,rsh->dcrh/dot_general | solution.py:25
  51.8 8.8 %copy.54 = bf16[16,2,1024,128]{3,2,1,0:T(8,128)(2,1)} copy(bf16[16,2,1024,128]{3,0,2,1:T(8,128)(2,1)} %convolution_convert_fusion.1) | data formatting | bytes 16777216 | tf_op jit(solution)/shard_map/convert_element_type | solution.py:27
  60.6 0.0 all-to-all-done
  60.6 7.2 %all-to-all-start.1 = ((bf16[16,2,1024,128]{3,2,1,0:T(8,128)(2,1)}), bf16[16,2,1024,128]{3,2,1,0:T(8,128)(2,1)}, u32[]{:S(2)}, u32[]{:S(2)}) async-start(bf16[16,2,1024,128]{3,2,1,0:T(8,128)(2,1)} %copy.54), calls=%async_computation.1 | async-start | bytes 16777216 | tf_op jit(solution)/shard_map/all_to_all | solution.py:72
  67.8 0.2 all-gather.2.cloned.1.call-start
  68.1 0.5 broadcast.270
  68.6 0.7 reduce.9
  69.3 0.1 eq.91
  69.3 118.5 %all-to-all-done.1 = bf16[16,2,1024,128]{3,2,1,0:T(8,128)(2,1)} async-done(((bf16[16,2,1024,128]{3,2,1,0:T(8,128)(2,1)}), bf16[16,2,1024,128]{3,2,1,0:T(8,128)(2,1)}, u32[]{:S(2)}, u32[]{:S(2)}) %all-to-all-start.1) | async-done | bytes 8388640 | tf_op jit(solution)/shard_map/all_to_all | solution.py:72
  187.9 9.3 %convert_bitcast_fusion.1 = bf16[1024,8,128]{2,1,0:T(8,128)(2,1)} fusion(bf16[32,1024,128]{2,1,0:T(8,128)(2,1)} %bitcast.10, s32[32]{0:T(128)S(1)} %eq.91), kind=kOutput, calls=%fused_computation.31 | convolution fusion | flops 68157696 | bytes 10485888 | tf_op jit(solution)/shard_map/ik,irh->rkh/dot_general | solution.py:80
  197.2 0.0 all-gather.2.cloned.1.call-update
  197.2 0.0 copy-done
  197.2 0.0 copy-start.7
  197.3 0.0 copy-start.8
  197.3 4.0 convert_bitcast_fusion
  201.2 0.1 convert_reduce_fusion
  201.3 18.2 %all-gather.2.cloned.1.call-done = bf16[1024,8,256]{2,1,0:T(8,128)(2,1)} async-done(((bf16[1024,8,128]{2,1,0:T(8,128)(2,1)}), bf16[1024,8,256]{2,1,0:T(8,128)(2,1)}) %all-gather.2.cloned.1.call-update) | async-done | bytes 4194320 | tf_op jit(solution)/shard_map/all_gather | solution.py:84
  219.5 10.1 %fusion.15 = (f32[1024]{0:T(1024)S(1)}, f32[1024,8,128,1]{2,0,3,1:T(8,128)}) fusion(f32[8,128]{1,0:T(8,128)S(1)} %copy-done.7, f32[1024]{0:T(1024)S(1)} %copy-done.8, f32[8]{0:T(128)S(1)} %get-tuple-element.10, bf16[8,256,8,128]{3,2,1,0:T(8,128)(2,1)} %convert_bitcast_fusion, bf16[1024,8,256]{2,1,0:T(8,128)(2,1)} %all-gather.2.cloned.1.call-done), kind=kOutput, calls=%fused_computation.24 | convolution fusion | flops 4299160576 | bytes 12595232 | tf_op jit(solution)/shard_map/rkb,kblh->rlh/dot_general | solution.py:39
  229.6 62.6 %psum.21 = f32[1024]{0:T(1024)S(1)} all-reduce(f32[1024]{0:T(1024)S(1)} %get-tuple-element.13), channel_id=1, replica_groups=mesh['row'=8,'col'=16,'pan'=2] {'col','pan'}, use_global_device_ids=true, to_apply=%region_4.6 | all-reduce | flops 1024 | bytes 8192 | tf_op jit(solution)/shard_map/psum | solution.py:89
  292.2 0.0 copy-start.5
  292.2 3.3 multiply_reduce_fusion
  295.5 17.7 %all-reduce = (f32[8,128]{1,0:T(8,128)S(1)}, f32[8]{0:T(128)S(1)}) all-reduce(f32[8,128]{1,0:T(8,128)S(1)} %multiply_reduce_fusion, f32[8]{0:T(128)S(1)} %get-tuple-element.9), channel_id=1, replica_groups=mesh['row'=8,'col'=16,'pan'=2] {'row'}, use_global_device_ids=true, to_apply=%region_7.9 | all-reduce | flops 1032 | bytes 8256 | tf_op jit(solution)/shard_map/psum | solution.py:92
  313.2 0.1 select_divide_fusion
  313.3 3.8 multiply_convert_fusion
  317.2 6.3 %convolution_convert_fusion = bf16[32,1024,128]{2,0,1:T(8,128)(2,1)S(1)} fusion(bf16[1024,8,128]{2,0,1:T(8,128)(2,1)S(1)} %multiply_convert_fusion, s32[32]{0:T(128)S(1)} %eq.91), kind=kOutput, calls=%fused_computation.7 | convolution fusion | flops 71303424 | bytes 10485888 | tf_op jit(solution)/shard_map/ik,rkh->irh/dot_general | solution.py:95
  323.5 8.0 %copy.60 = bf16[16,2,1024,128]{3,1,2,0:T(2,128)(2,1)S(1)} copy(bf16[16,2,1024,128]{3,1,0,2:T(2,128)(2,1)S(1)} %bitcast.91) | data formatting | bytes 16777216 | tf_op jit(solution)/shard_map/reshape | solution.py:98
  331.5 0.0 copy-start.1
  331.5 98.3 %all_to_all.16 = bf16[16,2,1024,128]{3,1,2,0:T(2,128)(2,1)S(1)} all-to-all(bf16[16,2,1024,128]{3,1,2,0:T(2,128)(2,1)S(1)} %copy.60), channel_id=1, replica_groups=mesh['row'=8,'col'=16,'pan'=2] {'col'}, dimensions={0} | all-to-all | bytes 16777216 | tf_op jit(solution)/shard_map/all_to_all | solution.py:99
  429.9 6.0 %fusion.32 = bf16[1024,8,128]{2,1,0:T(8,128)(2,1)} fusion(bf16[16,2,1024,128]{3,1,2,0:T(2,128)(2,1)S(1)} %all_to_all.16, pred[2,8]{1,0:T(4,128)(4,1)S(1)} %iota_compare_fusion.4, pred[16,8]{0,1:T(8,128)(4,1)S(1)} %iota_compare_fusion.3), kind=kOutput, calls=%fused_computation.36 | convolution fusion | flops 68157696 | bytes 10485904 | tf_op jit(solution)/shard_map/dcs,dcrh->rsh/dot_general | solution.py:100
  (29 shorter events, 0.1 us)
Async XLA Ops:
  7.2 190.1 %copy-start = (bf16[8,6,256,128]{3,2,1,0:T(8,128)(2,1)S(1)}, bf16[8,6,256,128]{3,2,1,0:T(8,128)(2,1)}, u32[]{:S(2)}) copy-start(bf16[8,6,256,128]{3,2,1,0:T(8,128)(2,1)} %param.16) | copy-start | bytes 9437188
  9.8 50.8 %all-to-all-start = ((s32[16,1,2]{2,1,0:T(1,128)}), s32[16,1,2]{2,1,0:T(1,128)S(1)}, u32[]{:S(2)}, u32[]{:S(2)}) async-start(s32[16,1,2]{2,1,0:T(1,128)} %copy.46), calls=%async_computation | async-start | bytes 16384 | tf_op jit(solution)/shard_map/all_to_all | solution.py:73
  33.3 2.8 copy-start.3
  33.3 2.8 copy-start.4
  36.2 1.6 copy-start.2
  60.6 127.3 %all-to-all-start.1 = ((bf16[16,2,1024,128]{3,2,1,0:T(8,128)(2,1)}), bf16[16,2,1024,128]{3,2,1,0:T(8,128)(2,1)}, u32[]{:S(2)}, u32[]{:S(2)}) async-start(bf16[16,2,1024,128]{3,2,1,0:T(8,128)(2,1)} %copy.54), calls=%async_computation.1 | async-start | bytes 16777216 | tf_op jit(solution)/shard_map/all_to_all | solution.py:72
  67.8 151.7 %all-gather.2.cloned.1.call-start = ((), (), s32[]{:S(2)}) async-start(), calls=%async_computation.3 | async-start | bytes 6291456 | tf_op jit(solution)/shard_map/all_gather | solution.py:84
  187.9 9.4 %copy-start.9 = (s32[8,6]{1,0:T(8,128)S(1)}, s32[8,6]{1,0:T(8,128)}, u32[]{:S(2)}) copy-start(s32[8,6]{1,0:T(8,128)} %param.17) | copy-start | bytes 580
  197.2 22.3 %copy-start.7 = (f32[8,128]{1,0:T(8,128)S(1)}, f32[8,128]{1,0:T(8,128)}, u32[]{:S(2)}) copy-start(f32[8,128]{1,0:T(8,128)} %param.21) | copy-start | bytes 12292
  197.3 22.3 %copy-start.8 = (f32[1024]{0:T(1024)S(1)}, f32[1024]{0:T(1024)}, u32[]{:S(2)}) copy-start(f32[1024]{0:T(1024)} %param.20) | copy-start | bytes 12292
  219.5 72.7 %copy-start.10 = (f32[1024]{0:T(1024)S(1)}, f32[1024]{0:T(1024)}, u32[]{:S(2)}) copy-start(f32[1024]{0:T(1024)} %param.18) | copy-start | bytes 12292
  229.6 83.6 %copy-start.11 = (f32[8,128]{1,0:T(8,128)S(1)}, f32[8,128]{1,0:T(8,128)}, u32[]{:S(2)}) copy-start(f32[8,128]{1,0:T(8,128)} %param.19) | copy-start | bytes 12292
  292.2 24.9 %copy-start.5 = (f32[1024]{0:T(1024)}, f32[1024]{0:T(1024)S(1)}, u32[]{:S(2)}) copy-start(f32[1024]{0:T(1024)S(1)} %multiply_divide_fusion) | copy-start | bytes 12292
  313.3 10.2 %copy-start.6 = (f32[8,128]{1,0:T(8,128)}, f32[8,128]{1,0:T(8,128)S(1)}, u32[]{:S(2)}) copy-start(f32[8,128]{1,0:T(8,128)S(1)} %select_divide_fusion) | copy-start | bytes 12292
  331.5 104.3 %copy-start.1 = (bf16[8,6,256,128]{3,2,1,0:T(8,128)(2,1)S(1)}, bf16[8,6,256,128]{3,2,1,0:T(8,128)(2,1)}, u32[]{:S(2)}) copy-start(bf16[8,6,256,128]{3,2,1,0:T(8,128)(2,1)} %param.16) | copy-start | bytes 9437188
Sparse Core Ops, SparseCore 0:
  197.3 22.1 all-gather.1
where the time goes:
time: 443 us
  blocking collectives  179 us (40%)
  waiting for transfers between devices  137 us (31%)
  matrix products  47.4 us (11%)
  local copies, waits for them, and re-layouts  40.8 us (9%)
  starting transfers between devices  14.9 us (3%)
  between operations  14.3 us (3%)
  other arithmetic  10 us (2%)
    all_to_all x1, waiting for transfers between devices, local(): lax.all_to_all(outgoing, 'col', split_axis=0, concat_axis=0, tiled=True)  119 us
    all_to_all x1, blocking collectives, local(): lax.all_to_all(returned, 'col', split_axis=0, concat_axis=0, tiled=True)  98.3 us
    psum x1, blocking collectives, local(): row_totals = lax.psum(jnp.sum(kernel_values, axis=(1, 2)), ('col', 'pan'))  62.6 us
    all_gather x1, waiting for transfers between devices, local(): gathered = lax.all_gather(dense_plan, 'pan', axis=2, tiled=True)  18.2 us
    psum x1, blocking collectives, local(): lax.psum((jnp.sum(weighted, axis=0), present * float(panel_rows)), 'row')  17.7 us
    gather x3, local copies, waits for them, and re-layouts, first_product(): picked = jnp.take(row_tiles, first_blocks[:, neighbor], axis=0)  10.8 us
    dot_general x1, matrix products, second_product(): jnp.einsum('rkb,kblh->rlh', dense_plan, panel_matrix, preferred_element_t...  10.1 us
    dot_general x1, matrix products, local(): jnp.einsum('ik,irh->rkh', matcher, arrivals, preferred_element_type=jnp.f...  9.33 us
  transfers between devices with their start and end apart: 3, of which 2 were waited for; matrix products, arithmetic and copies ran while one was open for 11% of the time, Pallas kernels for 0%

commit v1 on v0

--- a/solution.py
+++ b/solution.py
@@ -86,7 +86,9 @@
     kernel_values = present[None, :, None] * jnp.exp(
         crossed - offset_first[:, None, None] - offset_second[None]
     )
-    row_totals = lax.psum(jnp.sum(kernel_values, axis=(1, 2)), ("col", "pan"))
+    row_totals = jnp.sum(kernel_values, axis=(1, 2))
+    for over in ("pan", "col"):
+        row_totals = lax.psum(row_totals, over)
     scale_first = weight_first * plan_width / row_totals
     weighted = kernel_values * scale_first[:, None, None]
     colsum, counts = lax.psum((jnp.sum(weighted, axis=0), present * float(panel_rows)), "row")

time: 443 us -> 415 us (0.937)
  blocking collectives: 179 us -> 150 us
    psum x1 -> x2, blocking collectives: 62.6 us -> 39.1 us  [local(): row_totals = lax.psum(row_totals, over)]
    all_to_all x1, blocking collectives: 98.3 us -> 93.6 us  [local(): lax.all_to_all(returned, 'col', split_axis=0, concat_axis=0, tiled=True)]
  transfers between devices with their start and end apart: 3 -> 3, of which waited for: 2 -> 2; matrix products, arithmetic and copies ran while one was open for 11% -> 12% of each run, Pallas kernels for 0% -> 0%
where the time goes in v1:
time: 415 us
  blocking collectives  150 us (36%)
  waiting for transfers between devices  137 us (33%)
  matrix products  47.4 us (11%)
  local copies, waits for them, and re-layouts  40.8 us (10%)
  starting transfers between devices  14.9 us (4%)
  between operations  14.3 us (3%)
  other arithmetic  10 us (2%)
    all_to_all x1, waiting for transfers between devices, local(): lax.all_to_all(outgoing, 'col', split_axis=0, concat_axis=0, tiled=True)  119 us
    all_to_all x1, blocking collectives, local(): lax.all_to_all(returned, 'col', split_axis=0, concat_axis=0, tiled=True)  93.6 us
    psum x2, blocking collectives, local(): row_totals = lax.psum(row_totals, over)  39.1 us
    all_gather x1, waiting for transfers between devices, local(): gathered = lax.all_gather(dense_plan, 'pan', axis=2, tiled=True)  18.2 us
    psum x1, blocking collectives, local(): lax.psum((jnp.sum(weighted, axis=0), present * float(panel_rows)), 'row')  17.7 us
    gather x3, local copies, waits for them, and re-layouts, first_product(): picked = jnp.take(row_tiles, first_blocks[:, neighbor], axis=0)  10.8 us
    dot_general x1, matrix products, second_product(): jnp.einsum('rkb,kblh->rlh', dense_plan, panel_matrix, preferred_element_t...  10.1 us
    dot_general x1, matrix products, local(): jnp.einsum('ik,irh->rkh', matcher, arrivals, preferred_element_type=jnp.f...  9.33 us
  transfers between devices with their start and end apart: 3, of which 2 were waited for; matrix products, arithmetic and copies ran while one was open for 12% of the time, Pallas kernels for 0%

profile of v1, /device:TPU:2, one launch (start us, length us, event | category | flops | bytes accessed | tf_op | source)
XLA Modules:
  0.0 414.6 jit_solution(5951725573588719254)
XLA Ops:
  7.2 0.0 copy-start
  7.2 0.8 fusion.59
  8.0 0.8 fusion.60
  8.8 0.1 iota_compare_fusion.3
  8.9 0.2 convert_reduce_fusion.1
  9.1 0.1 fusion.47
  9.2 0.7 copy.46
  9.8 7.5 %all-to-all-start = ((s32[16,1,2]{2,1,0:T(1,128)}), s32[16,1,2]{2,1,0:T(1,128)S(1)}, u32[]{:S(2)}, u32[]{:S(2)}) async-start(s32[16,1,2]{2,1,0:T(1,128)} %copy.46), calls=%async_computation | async-start | bytes 16384 | tf_op jit(solution)/shard_map/all_to_all | solution.py:73
  17.3 1.0 slice_reduce_fusion.1
  18.4 4.2 %reshape.172 = bf16[4,256,1024]{2,1,0:T(8,128)(2,1)} reshape(bf16[1024,8,128]{2,1,0:T(8,128)(2,1)} %param.12) | data formatting | bytes 4194304 | tf_op jit(solution)/shard_map/reshape | solution.py:14
  22.6 3.6 gather_fusion.1
  26.1 3.6 gather_fusion.2
  29.7 3.6 gather_fusion
  33.3 2.8 fusion.20
  36.2 1.0 fusion.22
  37.3 0.5 copy-done.2
  37.8 2.7 fusion.29
  40.5 4.0 copy.53
  44.5 2.2 copy.72
  46.7 5.1 %convolution_convert_fusion.1 = bf16[16,2,1024,128]{3,0,2,1:T(8,128)(2,1)} fusion(bf16[1024,8,128,1]{2,1,0,3:T(8,128)(2,1)S(1)} %bitcast.93, pred[2,8]{1,0:T(4,128)(4,1)S(1)} %iota_compare_fusion.4, pred[16,8]{0,1:T(8,128)(4,1)S(1)} %iota_compare_fusion.3), kind=kOutput, calls=%fused_computation.8 | convolution fusion | flops 71303424 | bytes 10485904 | tf_op jit(solution)/shard_map/dcs,rsh->dcrh/dot_general | solution.py:25
  51.8 8.8 %copy.54 = bf16[16,2,1024,128]{3,2,1,0:T(8,128)(2,1)} copy(bf16[16,2,1024,128]{3,0,2,1:T(8,128)(2,1)} %convolution_convert_fusion.1) | data formatting | bytes 16777216 | tf_op jit(solution)/shard_map/convert_element_type | solution.py:27
  60.6 0.0 all-to-all-done
  60.6 7.2 %all-to-all-start.1 = ((bf16[16,2,1024,128]{3,2,1,0:T(8,128)(2,1)}), bf16[16,2,1024,128]{3,2,1,0:T(8,128)(2,1)}, u32[]{:S(2)}, u32[]{:S(2)}) async-start(bf16[16,2,1024,128]{3,2,1,0:T(8,128)(2,1)} %copy.54), calls=%async_computation.1 | async-start | bytes 16777216 | tf_op jit(solution)/shard_map/all_to_all | solution.py:72
  67.8 0.2 all-gather.2.cloned.1.call-start
  68.1 0.5 broadcast.270
  68.6 0.7 reduce.9
  69.3 0.1 eq.91
  69.3 118.5 %all-to-all-done.1 = bf16[16,2,1024,128]{3,2,1,0:T(8,128)(2,1)} async-done(((bf16[16,2,1024,128]{3,2,1,0:T(8,128)(2,1)}), bf16[16,2,1024,128]{3,2,1,0:T(8,128)(2,1)}, u32[]{:S(2)}, u32[]{:S(2)}) %all-to-all-start.1) | async-done | bytes 8388640 | tf_op jit(solution)/shard_map/all_to_all | solution.py:72
  187.9 9.3 %convert_bitcast_fusion.1 = bf16[1024,8,128]{2,1,0:T(8,128)(2,1)} fusion(bf16[32,1024,128]{2,1,0:T(8,128)(2,1)} %bitcast.10, s32[32]{0:T(128)S(1)} %eq.91), kind=kOutput, calls=%fused_computation.31 | convolution fusion | flops 68157696 | bytes 10485888 | tf_op jit(solution)/shard_map/ik,irh->rkh/dot_general | solution.py:80
  197.2 0.0 all-gather.2.cloned.1.call-update
  197.2 0.0 copy-start.7
  197.3 0.0 copy-start.8
  197.3 4.0 convert_bitcast_fusion
  201.2 0.1 convert_reduce_fusion
  201.3 18.2 %all-gather.2.cloned.1.call-done = bf16[1024,8,256]{2,1,0:T(8,128)(2,1)} async-done(((bf16[1024,8,128]{2,1,0:T(8,128)(2,1)}), bf16[1024,8,256]{2,1,0:T(8,128)(2,1)}) %all-gather.2.cloned.1.call-update) | async-done | bytes 4194320 | tf_op jit(solution)/shard_map/all_gather | solution.py:84
  219.5 10.1 %fusion.15 = (f32[1024]{0:T(1024)S(1)}, f32[1024,8,128,1]{2,0,3,1:T(8,128)}) fusion(f32[8,128]{1,0:T(8,128)S(1)} %copy-done.7, f32[1024]{0:T(1024)S(1)} %copy-done.8, f32[8]{0:T(128)S(1)} %get-tuple-element.10, bf16[8,256,8,128]{3,2,1,0:T(8,128)(2,1)} %convert_bitcast_fusion, bf16[1024,8,256]{2,1,0:T(8,128)(2,1)} %all-gather.2.cloned.1.call-done), kind=kOutput, calls=%fused_computation.24 | convolution fusion | flops 4299160576 | bytes 12595232 | tf_op jit(solution)/shard_map/rkb,kblh->rlh/dot_general | solution.py:39
  229.6 2.6 psum.28
  232.2 36.6 %psum.29 = f32[1024]{0:T(1024)S(1)} all-reduce(f32[1024]{0:T(1024)S(1)} %psum.28), channel_id=1, replica_groups=mesh['row'=8,'col'=16,'pan'=2] {'col'}, use_global_device_ids=true, to_apply=%region_5.7 | all-reduce | flops 1024 | bytes 8192 | tf_op jit(solution)/shard_map/psum | solution.py:91
  268.8 0.0 copy-start.5
  268.8 3.3 multiply_reduce_fusion
  272.1 17.7 %all-reduce = (f32[8,128]{1,0:T(8,128)S(1)}, f32[8]{0:T(128)S(1)}) all-reduce(f32[8,128]{1,0:T(8,128)S(1)} %multiply_reduce_fusion, f32[8]{0:T(128)S(1)} %get-tuple-element.9), channel_id=1, replica_groups=mesh['row'=8,'col'=16,'pan'=2] {'row'}, use_global_device_ids=true, to_apply=%region_8.10 | all-reduce | flops 1032 | bytes 8256 | tf_op jit(solution)/shard_map/psum | solution.py:94
  289.8 0.1 select_divide_fusion
  289.9 3.8 multiply_convert_fusion
  293.7 6.3 %convolution_convert_fusion = bf16[32,1024,128]{2,0,1:T(8,128)(2,1)S(1)} fusion(bf16[1024,8,128]{2,0,1:T(8,128)(2,1)S(1)} %multiply_convert_fusion, s32[32]{0:T(128)S(1)} %eq.91), kind=kOutput, calls=%fused_computation.7 | convolution fusion | flops 71303424 | bytes 10485888 | tf_op jit(solution)/shard_map/ik,rkh->irh/dot_general | solution.py:97
  300.0 8.0 %copy.60 = bf16[16,2,1024,128]{3,1,2,0:T(2,128)(2,1)S(1)} copy(bf16[16,2,1024,128]{3,1,0,2:T(2,128)(2,1)S(1)} %bitcast.91) | data formatting | bytes 16777216 | tf_op jit(solution)/shard_map/reshape | solution.py:100
  308.1 0.0 copy-start.1
  308.1 93.6 %all_to_all.16 = bf16[16,2,1024,128]{3,1,2,0:T(2,128)(2,1)S(1)} all-to-all(bf16[16,2,1024,128]{3,1,2,0:T(2,128)(2,1)S(1)} %copy.60), channel_id=1, replica_groups=mesh['row'=8,'col'=16,'pan'=2] {'col'}, dimensions={0} | all-to-all | bytes 16777216 | tf_op jit(solution)/shard_map/all_to_all | solution.py:101
  401.8 6.0 %fusion.32 = bf16[1024,8,128]{2,1,0:T(8,128)(2,1)} fusion(bf16[16,2,1024,128]{3,1,2,0:T(2,128)(2,1)S(1)} %all_to_all.16, pred[2,8]{1,0:T(4,128)(4,1)S(1)} %iota_compare_fusion.4, pred[16,8]{0,1:T(8,128)(4,1)S(1)} %iota_compare_fusion.3), kind=kOutput, calls=%fused_computation.36 | convolution fusion | flops 68157696 | bytes 10485904 | tf_op jit(solution)/shard_map/dcs,dcrh->rsh/dot_general | solution.py:102
  (30 shorter events, 0.1 us)
Async XLA Ops:
  7.2 190.1 %copy-start = (bf16[8,6,256,128]{3,2,1,0:T(8,128)(2,1)S(1)}, bf16[8,6,256,128]{3,2,1,0:T(8,128)(2,1)}, u32[]{:S(2)}) copy-start(bf16[8,6,256,128]{3,2,1,0:T(8,128)(2,1)} %param.16) | copy-start | bytes 9437188
  9.8 50.8 %all-to-all-start = ((s32[16,1,2]{2,1,0:T(1,128)}), s32[16,1,2]{2,1,0:T(1,128)S(1)}, u32[]{:S(2)}, u32[]{:S(2)}) async-start(s32[16,1,2]{2,1,0:T(1,128)} %copy.46), calls=%async_computation | async-start | bytes 16384 | tf_op jit(solution)/shard_map/all_to_all | solution.py:73
  33.3 2.8 copy-start.3
  33.3 2.8 copy-start.4
  36.2 1.6 copy-start.2
  60.6 127.3 %all-to-all-start.1 = ((bf16[16,2,1024,128]{3,2,1,0:T(8,128)(2,1)}), bf16[16,2,1024,128]{3,2,1,0:T(8,128)(2,1)}, u32[]{:S(2)}, u32[]{:S(2)}) async-start(bf16[16,2,1024,128]{3,2,1,0:T(8,128)(2,1)} %copy.54), calls=%async_computation.1 | async-start | bytes 16777216 | tf_op jit(solution)/shard_map/all_to_all | solution.py:72
  67.8 151.7 %all-gather.2.cloned.1.call-start = ((), (), s32[]{:S(2)}) async-start(), calls=%async_computation.3 | async-start | bytes 6291456 | tf_op jit(solution)/shard_map/all_gather | solution.py:84
  187.9 9.4 %copy-start.9 = (s32[8,6]{1,0:T(8,128)S(1)}, s32[8,6]{1,0:T(8,128)}, u32[]{:S(2)}) copy-start(s32[8,6]{1,0:T(8,128)} %param.17) | copy-start | bytes 580
  197.2 22.3 %copy-start.7 = (f32[8,128]{1,0:T(8,128)S(1)}, f32[8,128]{1,0:T(8,128)}, u32[]{:S(2)}) copy-start(f32[8,128]{1,0:T(8,128)} %param.21) | copy-start | bytes 12292
  197.3 22.3 %copy-start.8 = (f32[1024]{0:T(1024)S(1)}, f32[1024]{0:T(1024)}, u32[]{:S(2)}) copy-start(f32[1024]{0:T(1024)} %param.20) | copy-start | bytes 12292
  219.5 49.2 %copy-start.10 = (f32[1024]{0:T(1024)S(1)}, f32[1024]{0:T(1024)}, u32[]{:S(2)}) copy-start(f32[1024]{0:T(1024)} %param.18) | copy-start | bytes 12292
  229.6 60.2 %copy-start.11 = (f32[8,128]{1,0:T(8,128)S(1)}, f32[8,128]{1,0:T(8,128)}, u32[]{:S(2)}) copy-start(f32[8,128]{1,0:T(8,128)} %param.19) | copy-start | bytes 12292
  268.8 24.9 %copy-start.5 = (f32[1024]{0:T(1024)}, f32[1024]{0:T(1024)S(1)}, u32[]{:S(2)}) copy-start(f32[1024]{0:T(1024)S(1)} %multiply_divide_fusion) | copy-start | bytes 12292
  289.9 10.2 %copy-start.6 = (f32[8,128]{1,0:T(8,128)}, f32[8,128]{1,0:T(8,128)S(1)}, u32[]{:S(2)}) copy-start(f32[8,128]{1,0:T(8,128)S(1)} %select_divide_fusion) | copy-start | bytes 12292
  308.1 99.6 %copy-start.1 = (bf16[8,6,256,128]{3,2,1,0:T(8,128)(2,1)S(1)}, bf16[8,6,256,128]{3,2,1,0:T(8,128)(2,1)}, u32[]{:S(2)}) copy-start(bf16[8,6,256,128]{3,2,1,0:T(8,128)(2,1)} %param.16) | copy-start | bytes 9437188
Sparse Core Ops, SparseCore 0:
  197.3 22.1 all-gather.1
